TPU v7x, 128 devices: a whole 4x4x4 slice. The times are simulated.
128 devices in a mesh: row: 8 (over x, z_hi), col: 16 (over y, z_lo, core).
Axes of the slice: x: 4, y: 4, z: 4 (z_hi: 2, z_lo: 2; z = z_hi * 2 + z_lo), core: 2. Of those that a mesh axis runs over, the one named last changes fastest.
Arguments:
- matrix: float32 [16384, 16384], P('row', 'col'), may hold values from -6 to 6
- factor_inverse: float32 [512, 512], replicated, may hold values from -0.25 to 0.25
- panel: int32 [1], replicated, may hold values from 0 to 31
- split_index: int32 [1], replicated, may hold values from 4096 to 12288
Outputs:
- halves: float32 [16384, 512], P('col')
All inputs are finite; a program needn't handle non-finite values.
Results may differ from a plain program's by a relative error of at most 0.000071.
Values sent between devices are 32-bit elements; how exact they have to be, the bound alone decides.
No kernel may reach another device: no remote copies, remote signals or barrier semaphores. Data moves between devices by JAX's collectives and lax.ppermute only.
A program may use at most 64 MiB of HBM per device.

v0:
```python
import jax
import jax.numpy as jnp
from jax import lax
from jax.sharding import PartitionSpec as P


def broadcast(x, axis, root):
    mine = lax.axis_index(axis) == root
    return lax.psum(jnp.where(mine, x, jnp.zeros_like(x)), axis)


def identity_rows(first, count, start, width):
    rows_global = first + jnp.arange(count, dtype=jnp.int32)
    return (rows_global[:, None] == start + jnp.arange(width, dtype=jnp.int32)[None, :]).astype(
        jnp.float32
    )


def per_device(matrix, factor_inverse, panel, split_index):
    rows_loc, cols_loc = matrix.shape
    width = factor_inverse.shape[0]
    ncol = lax.axis_size("col")
    nrow = lax.axis_size("row")
    order = cols_loc * ncol
    col_idx = lax.axis_index("col")
    row_idx = lax.axis_index("row")
    start = panel[0] * width
    owner = start // cols_loc
    offset = start - owner * cols_loc
    piece = lax.dynamic_slice_in_dim(matrix, offset, width, 1)
    columns = broadcast(piece, "col", owner)
    partial_value = lax.dot_general(
        matrix,
        columns,
        (((0,), (0,)), ((), ())),
        precision=lax.Precision.HIGHEST,
        preferred_element_type=jnp.float32,
    )
    gram = lax.psum(partial_value, "row") / order + identity_rows(
        col_idx * cols_loc, cols_loc, start, width
    )
    factor = lax.dot_general(
        gram,
        factor_inverse,
        (((1,), (1,)), ((), ())),
        precision=lax.Precision.HIGHEST,
        preferred_element_type=jnp.float32,
    )
    per_dev = rows_loc // ncol
    ratio = ncol // nrow
    col_rows = order // ncol
    mine = identity_rows(row_idx * rows_loc + col_idx * per_dev, per_dev, start, width)
    product = lax.psum_scatter(
        jnp.dot(
            matrix, factor, precision=lax.Precision.HIGHEST, preferred_element_type=jnp.float32
        ),
        "col",
        scatter_dimension=0,
        tiled=True,
    )
    projector = 0.5 * (mine + product)
    row_stack = lax.all_gather(projector, "col", axis=0, tiled=True)
    selected = lax.dynamic_slice_in_dim(row_stack, col_idx % ratio * col_rows, col_rows, 0)
    gathered = broadcast(selected, "row", col_idx // ratio)
    rows_global = col_idx * col_rows + jnp.arange(col_rows, dtype=jnp.int32)
    keep = (rows_global < order // 2) == (rows_global < split_index[0])
    return jnp.where(keep[:, None], gathered, jnp.float32(0.0))


def solution(mesh):
    placed = (P("row", "col"), P(), P(), P())
    return jax.shard_map(
        per_device, mesh=mesh, in_specs=placed, out_specs=P("col", None), check_vma=False
    )
```

profile of v0, /device:TPU:0, one launch (start us, length us, event | category | flops | bytes accessed | tf_op | source)
XLA Modules:
  0.0 554.6 jit_solution(17478450682226694974)
XLA Ops:
  6.5 0.0 copy-start
  6.5 0.0 all-reduce.4.cloned.1.call-start
  7.3 4.7 dynamic-slice_select_fusion
  12.0 0.0 all-reduce.4.cloned.1.call-update
  12.0 0.0 all-reduce.6.cloned.1.call-start
  12.0 133.4 %all-reduce.4.cloned.1.call-done = f32[2048,512]{1,0:T(8,128)} async-done(((f32[2048,512]{1,0:T(8,128)}), f32[2048,512]{1,0:T(8,128)}) %all-reduce.4.cloned.1.call-update) | async-done | bytes 4194320 | tf_op jit(solution)/shard_map/psum | solution.py:9
  145.5 18.0 %convolution_bitcast_fusion.1 = f32[1024,512]{0,1:T(8,128)} fusion(f32[2048,512]{1,0:T(8,128)} %all-reduce.4.cloned.1.call-done, f32[2048,1024]{1,0:T(8,128)} %param.4), kind=kOutput, calls=%fused_computation.8 | convolution fusion | flops 12884901888 | bytes 14680064 | tf_op jit(solution)/shard_map/dot_general | solution.py:32
  163.5 0.0 all-reduce.6.cloned.1.call-update
  163.5 0.2 reduce-scatter.2.cloned.1.call-start
  163.7 112.2 %all-reduce.6.cloned.1.call-done = f32[1024,512]{0,1:T(8,128)} async-done(((f32[1024,512]{0,1:T(8,128)}), f32[1024,512]{0,1:T(8,128)}) %all-reduce.6.cloned.1.call-update) | async-done | bytes 2097168 | tf_op jit(solution)/shard_map/psum | solution.py:39
  276.0 0.0 copy-done
  276.0 8.4 %fusion = f32[1024,512]{1,0:T(8,128)S(1)} fusion(f32[512,512]{1,0:T(8,128)S(1)} %copy-done, f32[1024,512]{0,1:T(8,128)} %all-reduce.6.cloned.1.call-done, s32[1024]{0:T(1024)S(1)} %iota_add_fusion, s32[512]{0:T(512)S(1)} %iota_add_fusion.1), kind=kOutput, calls=%fused_computation.3 | convolution fusion | flops 3223322624 | bytes 5249024 | tf_op jit(solution)/shard_map/dot_general | solution.py:42
  284.4 31.0 %convolution_bitcast_fusion = f32[2048,512]{0,1:T(8,128)} fusion(f32[1024,512]{1,0:T(8,128)S(1)} %fusion, f32[2048,1024]{1,0:T(8,128)} %param.4), kind=kOutput, calls=%fused_computation.1 | convolution fusion | flops 12884901888 | bytes 14680064 | tf_op jit(solution)/shard_map/dot_general | solution.py:54
  315.4 0.0 reduce-scatter.2.cloned.1.call-update
  315.4 0.0 all-gather.2.cloned.1.call-start
  315.5 67.4 %reduce-scatter.2.cloned.1.call-done = f32[128,512]{0,1:T(8,128)} async-done(((f32[2048,512]{0,1:T(8,128)}), f32[128,512]{0,1:T(8,128)}) %reduce-scatter.2.cloned.1.call-update) | async-done | bytes 262160 | tf_op jit(solution)/shard_map/reduce_scatter | solution.py:53
  382.9 1.8 add_multiply_fusion
  384.6 0.0 all-gather.2.cloned.1.call-update
  384.7 0.0 all-reduce.8.cloned.1.call-start
  384.8 43.7 %all-gather.2.cloned.1.call-done = f32[2048,512]{0,1:T(8,128)} async-done(((f32[128,512]{0,1:T(8,128)}), f32[2048,512]{0,1:T(8,128)}) %all-gather.2.cloned.1.call-update) | async-done | bytes 4194320 | tf_op jit(solution)/shard_map/all_gather | solution.py:62
  428.5 3.2 dynamic-slice_select_fusion.1
  431.7 0.0 all-reduce.8.cloned.1.call-update
  432.4 112.1 %all-reduce.8.cloned.1.call-done = f32[1024,512]{0,1:T(8,128)} async-done(((f32[1024,512]{0,1:T(8,128)}), f32[1024,512]{0,1:T(8,128)}) %all-reduce.8.cloned.1.call-update) | async-done | bytes 2097168 | tf_op jit(solution)/shard_map/psum | solution.py:9
  544.5 1.8 broadcast_select_fusion
  546.3 1.8 copy.5
  (4 shorter events, 0.0 us)
Async XLA Ops:
  6.5 269.4 %copy-start = (f32[512,512]{1,0:T(8,128)S(1)}, f32[512,512]{1,0:T(8,128)}, u32[]{:S(2)}) copy-start(f32[512,512]{1,0:T(8,128)} %param.5) | copy-start | bytes 3145732
  6.5 138.9 %all-reduce.4.cloned.1.call-start = ((), (), s32[]{:S(2)}) async-start(), calls=%async_computation.1 | async-start | bytes 8388608 | tf_op jit(solution)/shard_map/psum | solution.py:9
  12.0 264.0 %all-reduce.6.cloned.1.call-start = ((), (), s32[]{:S(2)}) async-start(), calls=%async_computation.2 | async-start | bytes 4194304 | tf_op jit(solution)/shard_map/psum | solution.py:39
  163.5 219.4 %reduce-scatter.2.cloned.1.call-start = ((), (), s32[]{:S(2)}) async-start(), calls=%async_computation.3 | async-start | bytes 4456448 | tf_op jit(solution)/shard_map/reduce_scatter | solution.py:53
  315.4 113.1 %all-gather.2.cloned.1.call-start = ((), (), s32[]{:S(2)}) async-start(), calls=%async_computation.4 | async-start | bytes 4456448 | tf_op jit(solution)/shard_map/all_gather | solution.py:62
  384.7 159.8 %all-reduce.8.cloned.1.call-start = ((), (), s32[]{:S(2)}) async-start(), calls=%async_computation.5 | async-start | bytes 4194304 | tf_op jit(solution)/shard_map/psum | solution.py:9
Sparse Core Ops, SparseCore 0:
  12.1 133.3 all-reduce.3
  163.6 112.3 all-reduce.5
  315.5 67.3 reduce-scatter.1
  384.8 43.6 all-gather.1
  431.8 112.6 all-reduce.7
where the time goes:
time: 555 us
  waiting for transfers between devices  469 us (85%)
  matrix products  57.4 us (10%)
  between operations  14.6 us (3%)
  other arithmetic  11.4 us (2%)
    psum x2, waiting for transfers between devices, broadcast(): return lax.psum(jnp.where(mine, x, jnp.zeros_like(x)), axis)  246 us
    psum x1, waiting for transfers between devices, per_device(): lax.psum(partial_value, 'row') / order  112 us
    reduce_scatter x1, waiting for transfers between devices, per_device(): lax.psum_scatter(jnp.dot(matrix, factor, precision=lax.Precision.HIGHEST,...  67.4 us
    all_gather x1, waiting for transfers between devices, per_device(): row_stack = lax.all_gather(projector, 'col', axis=0, tiled=True)  43.7 us
    dot_general x1, matrix products, per_device(): jnp.dot(matrix, factor, precision=lax.Precision.HIGHEST, preferred_elemen...  31 us
    dot_general x1, matrix products, per_device(): lax.dot_general(matrix, columns, (((0,), (0,)), ((), ())), precision=lax....  18 us
  transfers between devices with their start and end apart: 5, of which 5 were waited for; matrix products, arithmetic and copies ran while one was open for 0% of the time, Pallas kernels for 0%

commit v1 on v0

--- a/solution.py
+++ b/solution.py
@@ -36,7 +36,7 @@
         precision=lax.Precision.HIGHEST,
         preferred_element_type=jnp.float32,
     )
-    gram = lax.psum(partial_value, "row") / order + identity_rows(
+    gram = jnp.sum(lax.all_gather(partial_value, "row"), axis=0) / order + identity_rows(
         col_idx * cols_loc, cols_loc, start, width
     )
     factor = lax.dot_general(

time: 555 us -> 651 us (1.17)
  waiting for transfers between devices: 469 us -> 541 us
  local copies, waits for them, and re-layouts: 1.82 us -> 21.5 us
    all_gather x0 -> x1, waiting for transfers between devices: none -> 186 us  [per_device(): lax.all_gather(partial_value, 'row')]
    psum x1 -> x0, waiting for transfers between devices: 112 us -> none  [per_device(): lax.psum(partial_value, 'row') / order]
    unnamed x2 -> x3, local copies, waits for them, and re-layouts: 0.01 us -> 19.7 us
where the time goes in v1:
time: 651 us; the launch traced here: 650 us
  waiting for transfers between devices  541 us (83%)
  matrix products  55.8 us (9%)
  local copies, waits for them, and re-layouts  21.5 us (3%)
  other arithmetic  17 us (3%)
  between operations  14.7 us (2%)
    psum x2, waiting for transfers between devices, broadcast(): return lax.psum(jnp.where(mine, x, jnp.zeros_like(x)), axis)  246 us
    all_gather x1, waiting for transfers between devices, per_device(): lax.all_gather(partial_value, 'row')  186 us
    reduce_scatter x1, waiting for transfers between devices, per_device(): lax.psum_scatter(jnp.dot(matrix, factor, precision=lax.Precision.HIGHEST,...  66 us
    all_gather x1, waiting for transfers between devices, per_device(): row_stack = lax.all_gather(projector, 'col', axis=0, tiled=True)  43.8 us
    dot_general x1, matrix products, per_device(): jnp.dot(matrix, factor, precision=lax.Precision.HIGHEST, preferred_elemen...  31 us
    unnamed x3, local copies, waits for them, and re-layouts  19.7 us
    dot_general x1, matrix products, per_device(): lax.dot_general(matrix, columns, (((0,), (0,)), ((), ())), precision=lax....  18 us
  transfers between devices with their start and end apart: 5, of which 5 were waited for; matrix products, arithmetic and copies ran while one was open for 0% of the time, Pallas kernels for 0%

profile of v1, /device:TPU:0, one launch (start us, length us, event | category | flops | bytes accessed | tf_op | source)
XLA Modules:
  0.0 650.4 jit_solution(16842085734590490022)
XLA Ops:
  6.5 0.0 copy-start
  6.5 0.0 all-reduce.3.cloned.1.call-start
  7.3 4.7 dynamic-slice_select_fusion
  12.0 0.0 all-reduce.3.cloned.1.call-update
  12.0 0.0 all-gather.6.cloned.1.call-start
  12.0 133.4 %all-reduce.3.cloned.1.call-done = f32[2048,512]{1,0:T(8,128)} async-done(((f32[2048,512]{1,0:T(8,128)}), f32[2048,512]{1,0:T(8,128)}) %all-reduce.3.cloned.1.call-update) | async-done | bytes 4194320 | tf_op jit(solution)/shard_map/psum | solution.py:9
  145.5 18.0 %convolution_bitcast_fusion.1 = f32[1024,512]{0,1:T(8,128)} fusion(f32[2048,512]{1,0:T(8,128)} %all-reduce.3.cloned.1.call-done, f32[2048,1024]{1,0:T(8,128)} %param.4), kind=kOutput, calls=%fused_computation.9 | convolution fusion | flops 12884901888 | bytes 14680064 | tf_op jit(solution)/shard_map/dot_general | solution.py:32
  163.5 0.0 all-gather.6.cloned.1.call-update
  163.5 0.2 reduce-scatter.2.cloned.1.call-start
  163.7 185.7 %all-gather.6.cloned.1.call-done = f32[8192,512]{0,1:T(8,128)} async-done(((f32[1024,512]{0,1:T(8,128)}), f32[8192,512]{0,1:T(8,128)}) %all-gather.6.cloned.1.call-update) | async-done | bytes 16777232 | tf_op jit(solution)/shard_map/all_gather | solution.py:39
  349.4 19.7 %copy.7 = f32[64,8,8,1024]{3,2,1,0:T(8,128)S(1)} copy(f32[64,8,8,1024]{3,1,2,0:T(8,128)} %bitcast.17) | data formatting | bytes 33554432
  369.1 5.6 bitcast_reduce_fusion
  374.7 0.0 copy-done
  374.7 6.8 %fusion = f32[1024,512]{1,0:T(8,128)S(1)} fusion(f32[512,512]{1,0:T(8,128)S(1)} %copy-done, f32[1024,512]{0,1:T(8,128)S(1)} %bitcast_reduce_fusion, s32[1024]{0:T(1024)S(1)} %iota_add_fusion, s32[512]{0:T(512)S(1)} %iota_add_fusion.1), kind=kOutput, calls=%fused_computation.4 | convolution fusion | flops 3223322624 | bytes 5249024 | tf_op jit(solution)/shard_map/dot_general | solution.py:42
  381.5 31.0 %convolution_bitcast_fusion = f32[2048,512]{0,1:T(8,128)} fusion(f32[1024,512]{1,0:T(8,128)S(1)} %fusion, f32[2048,1024]{1,0:T(8,128)} %param.4), kind=kOutput, calls=%fused_computation.2 | convolution fusion | flops 12884901888 | bytes 14680064 | tf_op jit(solution)/shard_map/dot_general | solution.py:54
  412.6 0.0 reduce-scatter.2.cloned.1.call-update
  412.6 0.0 all-gather.4.cloned.1.call-start
  412.7 66.0 %reduce-scatter.2.cloned.1.call-done = f32[128,512]{0,1:T(8,128)} async-done(((f32[2048,512]{0,1:T(8,128)}), f32[128,512]{0,1:T(8,128)}) %reduce-scatter.2.cloned.1.call-update) | async-done | bytes 262160 | tf_op jit(solution)/shard_map/reduce_scatter | solution.py:53
  478.6 1.8 add_multiply_fusion
  480.4 0.0 all-gather.4.cloned.1.call-update
  480.4 0.0 all-reduce.5.cloned.1.call-start
  480.5 43.8 %all-gather.4.cloned.1.call-done = f32[2048,512]{0,1:T(8,128)} async-done(((f32[128,512]{0,1:T(8,128)}), f32[2048,512]{0,1:T(8,128)}) %all-gather.4.cloned.1.call-update) | async-done | bytes 4194320 | tf_op jit(solution)/shard_map/all_gather | solution.py:62
  524.3 3.2 dynamic-slice_select_fusion.1
  527.5 0.0 all-reduce.5.cloned.1.call-update
  528.2 112.1 %all-reduce.5.cloned.1.call-done = f32[1024,512]{0,1:T(8,128)} async-done(((f32[1024,512]{0,1:T(8,128)}), f32[1024,512]{0,1:T(8,128)}) %all-reduce.5.cloned.1.call-update) | async-done | bytes 2097168 | tf_op jit(solution)/shard_map/psum | solution.py:9
  640.3 1.8 broadcast_select_fusion
  642.1 1.8 copy.6
  (4 shorter events, 0.0 us)
Async XLA Ops:
  6.5 368.2 %copy-start = (f32[512,512]{1,0:T(8,128)S(1)}, f32[512,512]{1,0:T(8,128)}, u32[]{:S(2)}) copy-start(f32[512,512]{1,0:T(8,128)} %param.5) | copy-start | bytes 3145732
  6.5 138.9 %all-reduce.3.cloned.1.call-start = ((), (), s32[]{:S(2)}) async-start(), calls=%async_computation.1 | async-start | bytes 8388608 | tf_op jit(solution)/shard_map/psum | solution.py:9
  12.0 337.4 %all-gather.6.cloned.1.call-start = ((), (), s32[]{:S(2)}) async-start(), calls=%async_computation.5 | async-start | bytes 18874368 | tf_op jit(solution)/shard_map/all_gather | solution.py:39
  163.5 315.1 %reduce-scatter.2.cloned.1.call-start = ((), (), s32[]{:S(2)}) async-start(), calls=%async_computation.2 | async-start | bytes 4456448 | tf_op jit(solution)/shard_map/reduce_scatter | solution.py:53
  412.6 111.7 %all-gather.4.cloned.1.call-start = ((), (), s32[]{:S(2)}) async-start(), calls=%async_computation.3 | async-start | bytes 4456448 | tf_op jit(solution)/shard_map/all_gather | solution.py:62
  480.4 159.9 %all-reduce.5.cloned.1.call-start = ((), (), s32[]{:S(2)}) async-start(), calls=%async_computation.4 | async-start | bytes 4194304 | tf_op jit(solution)/shard_map/psum | solution.py:9
Sparse Core Ops, SparseCore 0:
  12.1 133.3 all-reduce.2
  163.6 185.7 all-gather.5
  412.7 65.8 reduce-scatter.1
  480.6 43.6 all-gather.3
  527.6 112.6 all-reduce.4

commit v2 on v0

--- a/solution.py
+++ b/solution.py
@@ -59,7 +59,9 @@
         tiled=True,
     )
     projector = 0.5 * (mine + product)
-    row_stack = lax.all_gather(projector, "col", axis=0, tiled=True)
+    row_stack = jnp.concatenate(
+        lax.all_to_all(jnp.stack([projector] * lax.axis_size("col")), "col", 0, 0), axis=0
+    )
     selected = lax.dynamic_slice_in_dim(row_stack, col_idx % ratio * col_rows, col_rows, 0)
     gathered = broadcast(selected, "row", col_idx // ratio)
     rows_global = col_idx * col_rows + jnp.arange(col_rows, dtype=jnp.int32)

time: 555 us -> 576 us (1.038)
  waiting for transfers between devices: 469 us -> 484 us
    all_to_all x0 -> x1, waiting for transfers between devices: none -> 52 us  [per_device(): lax.all_to_all(jnp.stack([projector] * lax.axis_size('col')), 'col', 0, 0)]
    all_gather x1 -> x0, waiting for transfers between devices: 43.7 us -> none  [per_device(): row_stack = lax.all_gather(projector, 'col', axis=0, tiled=True)]
    psum x2, waiting for transfers between devices: 246 us -> 252 us  [broadcast(): return lax.psum(jnp.where(mine, x, jnp.zeros_like(x)), axis)]
where the time goes in v2:
time: 576 us; the launch traced here: 575 us
  waiting for transfers between devices  484 us (84%)
  matrix products  57.3 us (10%)
  between operations  14.7 us (3%)
  other arithmetic  12 us (2%)
    psum x2, waiting for transfers between devices, broadcast(): return lax.psum(jnp.where(mine, x, jnp.zeros_like(x)), axis)  252 us
    psum x1, waiting for transfers between devices, per_device(): lax.psum(partial_value, 'row') / order  113 us
    reduce_scatter x1, waiting for transfers between devices, per_device(): lax.psum_scatter(jnp.dot(matrix, factor, precision=lax.Precision.HIGHEST,...  67.4 us
    all_to_all x1, waiting for transfers between devices, per_device(): lax.all_to_all(jnp.stack([projector] * lax.axis_size('col')), 'col', 0, 0)  52 us
    dot_general x1, matrix products, per_device(): jnp.dot(matrix, factor, precision=lax.Precision.HIGHEST, preferred_elemen...  30.9 us
    dot_general x1, matrix products, per_device(): lax.dot_general(matrix, columns, (((0,), (0,)), ((), ())), precision=lax....  18 us
  transfers between devices with their start and end apart: 5, of which 5 were waited for; matrix products, arithmetic and copies ran while one was open for 0% of the time, Pallas kernels for 0%

profile of v2, /device:TPU:0, one launch (start us, length us, event | category | flops | bytes accessed | tf_op | source)
XLA Modules:
  0.0 575.4 jit_solution(2759552142055198964)
XLA Ops:
  6.5 0.0 copy-start
  6.5 0.0 all-reduce.4.cloned.1.call-start
  7.3 4.7 dynamic-slice_select_fusion
  12.0 0.0 all-reduce.4.cloned.1.call-update
  12.0 0.0 all-reduce.6.cloned.1.call-start
  12.0 133.4 %all-reduce.4.cloned.1.call-done = f32[2048,512]{1,0:T(8,128)} async-done(((f32[2048,512]{1,0:T(8,128)}), f32[2048,512]{1,0:T(8,128)}) %all-reduce.4.cloned.1.call-update) | async-done | bytes 4194320 | tf_op jit(solution)/shard_map/psum | solution.py:9
  145.5 18.0 %convolution_bitcast_fusion.1 = f32[1024,512]{0,1:T(8,128)} fusion(f32[2048,512]{1,0:T(8,128)} %all-reduce.4.cloned.1.call-done, f32[2048,1024]{1,0:T(8,128)} %param.4), kind=kOutput, calls=%fused_computation.8 | convolution fusion | flops 12884901888 | bytes 14680064 | tf_op jit(solution)/shard_map/dot_general | solution.py:32
  163.5 0.0 all-reduce.6.cloned.1.call-update
  163.5 0.2 reduce-scatter.2.cloned.1.call-start
  163.7 112.5 %all-reduce.6.cloned.1.call-done = f32[1024,512]{0,1:T(8,128)} async-done(((f32[1024,512]{0,1:T(8,128)}), f32[1024,512]{0,1:T(8,128)}) %all-reduce.6.cloned.1.call-update) | async-done | bytes 2097168 | tf_op jit(solution)/shard_map/psum | solution.py:39
  276.3 0.0 copy-done
  276.3 8.4 %fusion = f32[1024,512]{1,0:T(8,128)S(1)} fusion(f32[512,512]{1,0:T(8,128)S(1)} %copy-done, f32[1024,512]{0,1:T(8,128)} %all-reduce.6.cloned.1.call-done, s32[1024]{0:T(1024)S(1)} %iota_add_fusion, s32[512]{0:T(512)S(1)} %iota_add_fusion.1), kind=kOutput, calls=%fused_computation.3 | convolution fusion | flops 3223322624 | bytes 5249024 | tf_op jit(solution)/shard_map/dot_general | solution.py:42
  284.7 30.9 %convolution_bitcast_fusion = f32[2048,512]{0,1:T(8,128)} fusion(f32[1024,512]{1,0:T(8,128)S(1)} %fusion, f32[2048,1024]{1,0:T(8,128)} %param.4), kind=kOutput, calls=%fused_computation.1 | convolution fusion | flops 12884901888 | bytes 14680064 | tf_op jit(solution)/shard_map/dot_general | solution.py:54
  315.6 0.0 reduce-scatter.2.cloned.1.call-update
  315.7 67.4 %reduce-scatter.2.cloned.1.call-done = f32[128,512]{0,1:T(8,128)} async-done(((f32[2048,512]{0,1:T(8,128)}), f32[128,512]{0,1:T(8,128)}) %reduce-scatter.2.cloned.1.call-update) | async-done | bytes 262160 | tf_op jit(solution)/shard_map/reduce_scatter | solution.py:53
  383.1 1.1 add_multiply_fusion
  384.1 0.1 copy.5
  384.3 2.5 stack.2
  386.8 4.5 all-to-all-start
  391.3 0.0 all-reduce.8.cloned.1.call-start
  391.4 52.0 %all-to-all-done = f32[16,128,512]{2,1,0:T(8,128)} async-done(((f32[16,128,512]{2,1,0:T(8,128)}), f32[16,128,512]{2,1,0:T(8,128)}, u32[]{:S(2)}, u32[]{:S(2)}) %all-to-all-start) | async-done | bytes 4194336 | tf_op jit(solution)/shard_map/all_to_all | solution.py:63
  443.5 3.1 dynamic-slice_select_fusion.1
  446.6 0.0 all-reduce.8.cloned.1.call-update
  447.3 118.5 %all-reduce.8.cloned.1.call-done = f32[1024,512]{1,0:T(8,128)} async-done(((f32[1024,512]{1,0:T(8,128)}), f32[1024,512]{1,0:T(8,128)}) %all-reduce.8.cloned.1.call-update) | async-done | bytes 2097168 | tf_op jit(solution)/shard_map/psum | solution.py:9
  565.8 3.1 broadcast_select_fusion
  (4 shorter events, 0.0 us)
Async XLA Ops:
  6.5 269.7 %copy-start = (f32[512,512]{1,0:T(8,128)S(1)}, f32[512,512]{1,0:T(8,128)}, u32[]{:S(2)}) copy-start(f32[512,512]{1,0:T(8,128)} %param.5) | copy-start | bytes 3145732
  6.5 138.9 %all-reduce.4.cloned.1.call-start = ((), (), s32[]{:S(2)}) async-start(), calls=%async_computation.2 | async-start | bytes 8388608 | tf_op jit(solution)/shard_map/psum | solution.py:9
  12.0 264.3 %all-reduce.6.cloned.1.call-start = ((), (), s32[]{:S(2)}) async-start(), calls=%async_computation.3 | async-start | bytes 4194304 | tf_op jit(solution)/shard_map/psum | solution.py:39
  163.5 219.6 %reduce-scatter.2.cloned.1.call-start = ((), (), s32[]{:S(2)}) async-start(), calls=%async_computation.4 | async-start | bytes 4456448 | tf_op jit(solution)/shard_map/reduce_scatter | solution.py:53
  386.8 56.7 %all-to-all-start = ((f32[16,128,512]{2,1,0:T(8,128)}), f32[16,128,512]{2,1,0:T(8,128)}, u32[]{:S(2)}, u32[]{:S(2)}) async-start(f32[16,128,512]{2,1,0:T(8,128)} %stack.2), calls=%async_computation.1 | async-start | bytes 8388608 | tf_op jit(solution)/shard_map/all_to_all | solution.py:63
  391.3 174.4 %all-reduce.8.cloned.1.call-start = ((), (), s32[]{:S(2)}) async-start(), calls=%async_computation.5 | async-start | bytes 4194304 | tf_op jit(solution)/shard_map/psum | solution.py:9
Sparse Core Ops, SparseCore 0:
  12.1 133.3 all-reduce.3
  163.6 112.6 all-reduce.5
  315.8 67.2 reduce-scatter.1
  446.7 118.9 all-reduce.7
